TPU v7x, 128 devices: a whole 4x4x4 slice. The times are simulated.
128 devices in a mesh: ublk: 16 (over x, z), salt: 8 (over y, core).
Axes of the slice: x: 4, y: 4, z: 4, core: 2. Of those that a mesh axis runs over, the one named last changes fastest.
Arguments:
- user_factors: bfloat16 [16, 8192, 256], P('ublk', 'salt')
- tile_users: int32 [16, 8, 4096], P('ublk', 'salt'), may hold values from 0 to 8191
- tile_items: int32 [16, 8, 4096], P('ublk', 'salt'), may hold values from 0 to 511
- tile_weight: float32 [16, 8, 4096], P('ublk', 'salt'), may hold values from 0.5 to 8
- live_count: int32 [16, 8], P('ublk', 'salt'), may hold values from 2048 to 4096, as said below
Outputs:
- item_factors: float32 [8, 512, 256], P('salt', 'ublk')
- residual: float32 [8, 512, 256], P('salt', 'ublk')
Inputs may be any that keep to these rules, and one draw needn't show every extreme that they name: Every entry of live_count is at least 2048 and at most 4096; some tile is full.
All inputs are finite; a program needn't handle non-finite values.
Results may differ from a plain program's by a relative error of at most 0.0022.
Values may be sent and summed in bfloat16 or wider, within the bound.
A program may use at most 64 MiB of HBM per device.

v0:
```python
import jax
import jax.numpy as jnp
from jax import lax
from jax.sharding import PartitionSpec as P

ITERS = 8
ITEM_DEV = 32
REG = 1.0
EPS = 1e-06


def conjugate(rhs, image_of):
    solution = jnp.zeros_like(rhs)
    resid = rhs
    direction = rhs
    norm_now = jnp.sum(resid * resid, axis=1)
    for step in range(ITERS):
        image = image_of(direction)
        alpha = norm_now / (jnp.sum(direction * image, axis=1) + EPS)
        solution = solution + alpha[:, None] * direction
        resid = resid - alpha[:, None] * image
        norm_next = jnp.sum(resid * resid, axis=1)
        direction = resid + (norm_next / (norm_now + EPS))[:, None] * direction
        norm_now = norm_next
    return (solution, resid)


def body(user_factors, tile_users, tile_items, tile_weight, live_count):
    shard = user_factors[0]
    block = lax.all_gather(shard, "salt", axis=0, tiled=True)
    contract = (((0,), (0,)), ((), ()))
    own_gram = lax.dot_general(shard, shard, contract, preferred_element_type=jnp.float32)
    gram = lax.psum(own_gram, ("ublk", "salt"))
    users = tile_users[0, 0]
    items = tile_items[0, 0]
    raw = tile_weight[0, 0]
    live = jnp.arange(users.shape[0], dtype=jnp.int32) < live_count[0, 0]
    weight = jnp.where(live, raw, jnp.zeros_like(raw))
    confid = jnp.where(live, 1.0 + raw, jnp.zeros_like(raw))
    rows = jnp.take(block, users, axis=0).astype(jnp.float32)
    column_items = ITEM_DEV * lax.axis_size("ublk")
    rhs_terms = jax.ops.segment_sum(confid[:, None] * rows, items, num_segments=column_items)

    def local_terms(whole_dir):
        along = jnp.sum(rows * whole_dir[items], axis=1) * weight
        return jax.ops.segment_sum(along[:, None] * rows, items, num_segments=column_items)

    def finish(summed, direction):
        return summed + jnp.dot(direction, gram, precision=lax.Precision.HIGHEST) + REG * direction

    rhs = lax.psum(rhs_terms, "ublk")

    def image_every(direction):
        summed = lax.psum(local_terms(direction), "ublk")
        return finish(summed, direction)

    solution_all, resid_all = conjugate(rhs, image_every)
    start = lax.axis_index("ublk") * ITEM_DEV
    solution = lax.dynamic_slice_in_dim(solution_all, start, ITEM_DEV, 0)
    resid = lax.dynamic_slice_in_dim(resid_all, start, ITEM_DEV, 0)
    return (solution[None], resid[None])


def solution(mesh):
    return jax.shard_map(
        body,
        mesh=mesh,
        in_specs=(
            P("ublk", "salt", None),
            P("ublk", "salt", None),
            P("ublk", "salt", None),
            P("ublk", "salt", None),
            P("ublk", "salt"),
        ),
        out_specs=(P("salt", "ublk", None), P("salt", "ublk", None)),
        check_vma=False,
    )
```

profile of v0, /device:TPU:0, one launch (start us, length us, event | category | flops | bytes accessed | tf_op | source)
XLA Modules:
  0.0 1352.9 jit_solution(7503660293953594438)
XLA Ops:
  10.8 33.5 %all-gather.3.cloned.1.call-done = bf16[1,8192,256]{2,1,0:T(8,128)(2,1)} async-done(((bf16[1,1024,256]{2,1,0:T(8,128)(2,1)}), bf16[1,8192,256]{2,1,0:T(8,128)(2,1)}) %all-gather.3.cloned.1.call-update) | async-done | bytes 4194320 | tf_op jit(solution)/shard_map/all_gather | solution.py:30
  60.1 26.1 %scatter_custom_fusion = f32[512,256]{1,0:T(8,128)} fusion(s32[4096]{0:T(1024)S(1)} %bitcast.56, f32[4096]{0:T(1024)S(1)} %add_select_fusion, f32[]{:T(128)} %constant.11.clone.1, bf16[4096,256]{1,0:T(8,128)(2,1)S(1)} %gather_fusion, pred[4096]{0:T(1024)(128)(4,1)S(1)} %compare_and_fusion), kind=kCustom, calls=%fused_computation.35 | custom fusion | flops 4194304 | bytes 2641924 | tf_op jit(solution)/shard_map/scatter-add | solution.py:42
  87.4 84.7 %all-reduce.11.cloned.1.call-done = f32[512,256]{1,0:T(8,128)} async-done(((f32[512,256]{1,0:T(8,128)}), f32[512,256]{1,0:T(8,128)}) %all-reduce.11.cloned.1.call-update) | async-done | bytes 524304 | tf_op jit(solution)/shard_map/psum | solution.py:51
  172.1 17.1 %gather_fusion.1 = f32[4096,256]{1,0:T(8,128)} fusion(f32[512,256]{1,0:T(8,128)} %all-reduce.11.cloned.1.call-done, s32[4096]{0:T(1024)S(1)} %broadcast_clamp_fusion), kind=kCustom, calls=%fused_computation.1 | custom fusion | bytes 8404992 | tf_op jit(solution)/shard_map/gather | solution.py:45
  192.2 26.1 %scatter_custom_fusion.1 = f32[512,256]{1,0:T(8,128)} fusion(s32[4096]{0:T(1024)S(1)} %bitcast.57, f32[4096]{0:T(1024)S(1)} %fusion.60, f32[]{:T(128)} %constant.11.clone.1, bf16[4096,256]{1,0:T(8,128)(2,1)S(1)} %gather_fusion, pred[4096]{0:T(1024)(128)(4,1)S(1)} %compare_and_fusion), kind=kCustom, calls=%fused_computation.37 | custom fusion | flops 4194304 | bytes 2641924 | tf_op jit(solution)/shard_map/scatter-add | solution.py:46
  218.7 100.7 %all-reduce.15.cloned.1.call-done = f32[256,256]{1,0:T(8,128)} async-done(((f32[256,256]{1,0:T(8,128)}), f32[256,256]{1,0:T(8,128)}) %all-reduce.15.cloned.1.call-update) | async-done | bytes 262160 | tf_op jit(solution)/shard_map/psum | solution.py:33
  319.4 86.2 %all-reduce.13.cloned.1.call-done = f32[512,256]{1,0:T(8,128)} async-done(((f32[512,256]{1,0:T(8,128)}), f32[512,256]{1,0:T(8,128)}) %all-reduce.13.cloned.1.call-update) | async-done | bytes 524304 | tf_op jit(solution)/shard_map/psum | solution.py:54
  408.4 16.1 %gather_fusion.2 = f32[4096,256]{1,0:T(8,128)} fusion(f32[512,256]{1,0:T(8,128)S(1)} %multiply_add_fusion.7, s32[4096]{0:T(1024)S(1)} %broadcast_clamp_fusion), kind=kCustom, calls=%fused_computation.2 | custom fusion | bytes 8404992 | tf_op jit(solution)/shard_map/gather | solution.py:45
  427.5 26.1 %scatter_custom_fusion.2 = f32[512,256]{1,0:T(8,128)} fusion(s32[4096]{0:T(1024)S(1)} %bitcast.58, f32[4096]{0:T(1024)S(1)} %fusion.59, f32[]{:T(128)} %constant.11.clone.1, bf16[4096,256]{1,0:T(8,128)(2,1)S(1)} %gather_fusion, pred[4096]{0:T(1024)(128)(4,1)S(1)} %compare_and_fusion), kind=kCustom, calls=%fused_computation.39 | custom fusion | flops 4194304 | bytes 2641924 | tf_op jit(solution)/shard_map/scatter-add | solution.py:46
  453.7 85.3 %all-reduce.17.cloned.1.call-done = f32[512,256]{1,0:T(8,128)} async-done(((f32[512,256]{1,0:T(8,128)}), f32[512,256]{1,0:T(8,128)}) %all-reduce.17.cloned.1.call-update) | async-done | bytes 524304 | tf_op jit(solution)/shard_map/psum | solution.py:54
  562.5 26.5 %scatter_custom_fusion.3 = f32[512,256]{1,0:T(8,128)} fusion(s32[4096]{0:T(1024)S(1)} %bitcast.59, f32[4096]{0:T(1024)S(1)} %fusion.58, f32[]{:T(128)} %constant.11.clone.1, bf16[4096,256]{1,0:T(8,128)(2,1)} %copy-done.1, pred[4096]{0:T(1024)(128)(4,1)S(1)} %compare_and_fusion), kind=kCustom, calls=%fused_computation.41 | custom fusion | flops 4194304 | bytes 2641924 | tf_op jit(solution)/shard_map/scatter-add | solution.py:46
  589.6 84.6 %all-reduce.19.cloned.1.call-done = f32[512,256]{1,0:T(8,128)} async-done(((f32[512,256]{1,0:T(8,128)}), f32[512,256]{1,0:T(8,128)}) %all-reduce.19.cloned.1.call-update) | async-done | bytes 524304 | tf_op jit(solution)/shard_map/psum | solution.py:54
  696.4 26.1 %scatter_custom_fusion.4 = f32[512,256]{1,0:T(8,128)} fusion(s32[4096]{0:T(1024)S(1)} %bitcast.60, f32[4096]{0:T(1024)S(1)} %fusion.57, f32[]{:T(128)} %constant.11.clone.1, bf16[4096,256]{1,0:T(8,128)(2,1)S(1)} %copy-done.2, pred[4096]{0:T(1024)(128)(4,1)S(1)} %compare_and_fusion), kind=kCustom, calls=%fused_computation.43 | custom fusion | flops 4194304 | bytes 2641924 | tf_op jit(solution)/shard_map/scatter-add | solution.py:46
  722.6 85.2 %all-reduce.21.cloned.1.call-done = f32[512,256]{1,0:T(8,128)} async-done(((f32[512,256]{1,0:T(8,128)}), f32[512,256]{1,0:T(8,128)}) %all-reduce.21.cloned.1.call-update) | async-done | bytes 524304 | tf_op jit(solution)/shard_map/psum | solution.py:54
  810.7 16.1 %gather_fusion.5 = f32[4096,256]{1,0:T(8,128)} fusion(f32[512,256]{1,0:T(8,128)S(1)} %multiply_add_fusion.3, s32[4096]{0:T(1024)S(1)} %broadcast_clamp_fusion), kind=kCustom, calls=%fused_computation.5 | custom fusion | bytes 8404992 | tf_op jit(solution)/shard_map/gather | solution.py:45
  829.7 26.1 %scatter_custom_fusion.5 = f32[512,256]{1,0:T(8,128)} fusion(s32[4096]{0:T(1024)S(1)} %bitcast.61, f32[4096]{0:T(1024)S(1)} %fusion.56, f32[]{:T(128)} %constant.11.clone.1, bf16[4096,256]{1,0:T(8,128)(2,1)S(1)} %copy-done.2, pred[4096]{0:T(1024)(128)(4,1)S(1)} %compare_and_fusion), kind=kCustom, calls=%fused_computation.45 | custom fusion | flops 4194304 | bytes 2641924 | tf_op jit(solution)/shard_map/scatter-add | solution.py:46
  856.1 85.1 %all-reduce.23.cloned.1.call-done = f32[512,256]{1,0:T(8,128)} async-done(((f32[512,256]{1,0:T(8,128)}), f32[512,256]{1,0:T(8,128)}) %all-reduce.23.cloned.1.call-update) | async-done | bytes 524304 | tf_op jit(solution)/shard_map/psum | solution.py:54
  963.9 26.5 %scatter_custom_fusion.6 = f32[512,256]{1,0:T(8,128)} fusion(s32[4096]{0:T(1024)S(1)} %bitcast.62, f32[4096]{0:T(1024)S(1)} %fusion.55, f32[]{:T(128)} %constant.11.clone.1, bf16[4096,256]{1,0:T(8,128)(2,1)} %copy-done.1, pred[4096]{0:T(1024)(128)(4,1)S(1)} %compare_and_fusion), kind=kCustom, calls=%fused_computation.47 | custom fusion | flops 4194304 | bytes 2641924 | tf_op jit(solution)/shard_map/scatter-add | solution.py:46
  990.5 85.2 %all-reduce.25.cloned.1.call-done = f32[512,256]{1,0:T(8,128)} async-done(((f32[512,256]{1,0:T(8,128)}), f32[512,256]{1,0:T(8,128)}) %all-reduce.25.cloned.1.call-update) | async-done | bytes 524304 | tf_op jit(solution)/shard_map/psum | solution.py:54
  1077.9 16.1 %gather_fusion.7 = f32[4096,256]{1,0:T(8,128)} fusion(f32[512,256]{1,0:T(8,128)S(1)} %multiply_add_fusion.1, s32[4096]{0:T(1024)S(1)} %broadcast_clamp_fusion), kind=kCustom, calls=%fused_computation.7 | custom fusion | bytes 8404992 | tf_op jit(solution)/shard_map/gather | solution.py:45
  1097.5 26.5 %scatter_custom_fusion.7 = f32[512,256]{1,0:T(8,128)} fusion(s32[4096]{0:T(1024)S(1)} %bitcast.63, f32[4096]{0:T(1024)S(1)} %fusion.54, f32[]{:T(128)} %constant.11.clone.1, bf16[4096,256]{1,0:T(8,128)(2,1)} %copy-done.1, pred[4096]{0:T(1024)(128)(4,1)S(1)} %compare_and_fusion), kind=kCustom, calls=%fused_computation.49 | custom fusion | flops 4194304 | bytes 2641924 | tf_op jit(solution)/shard_map/scatter-add | solution.py:46
  1124.3 85.0 %all-reduce.27.cloned.1.call-done = f32[512,256]{1,0:T(8,128)} async-done(((f32[512,256]{1,0:T(8,128)}), f32[512,256]{1,0:T(8,128)}) %all-reduce.27.cloned.1.call-update) | async-done | bytes 524304 | tf_op jit(solution)/shard_map/psum | solution.py:54
  1231.0 26.5 %scatter_custom_fusion.8 = f32[512,256]{1,0:T(8,128)} fusion(s32[4096]{0:T(1024)S(1)} %bitcast.64, f32[4096]{0:T(1024)S(1)} %fusion.53, f32[]{:T(128)} %constant.11.clone.1, bf16[4096,256]{1,0:T(8,128)(2,1)} %copy-done.1, pred[4096]{0:T(1024)(128)(4,1)S(1)} %compare_and_fusion), kind=kCustom, calls=%fused_computation.51 | custom fusion | flops 4194304 | bytes 2641924 | tf_op jit(solution)/shard_map/scatter-add | solution.py:46
  1257.8 85.0 %all-reduce.29.cloned.1.call-done = f32[512,256]{1,0:T(8,128)} async-done(((f32[512,256]{1,0:T(8,128)}), f32[512,256]{1,0:T(8,128)}) %all-reduce.29.cloned.1.call-update) | async-done | bytes 524304 | tf_op jit(solution)/shard_map/psum | solution.py:54
  (115 shorter events, 135.3 us)
Async XLA Ops:
  7.2 37.1 %all-gather.3.cloned.1.call-start = ((), (), s32[]{:S(2)}) async-start(), calls=%async_computation.10 | async-start | bytes 4718592 | tf_op jit(solution)/shard_map/all_gather | solution.py:30
  7.9 164.2 %all-reduce.11.cloned.1.call-start = ((), (), s32[]{:S(2)}) async-start(), calls=%async_computation | async-start | bytes 1048576 | tf_op jit(solution)/shard_map/psum | solution.py:51
  44.3 15.8 %copy-start.10 = (s32[1,1,4096]{2,1,0:T(1,128)S(1)}, s32[1,1,4096]{2,1,0:T(1,128)}, u32[]{:S(2)}) copy-start(s32[1,1,4096]{2,1,0:T(1,128)} %param.7) | copy-start | bytes 49156
  44.3 42.0 %copy-start.9 = (bf16[1,1024,256]{2,1,0:T(8,128)(2,1)S(1)}, bf16[1,1024,256]{2,1,0:T(8,128)(2,1)}, u32[]{:S(2)}) copy-start(bf16[1,1024,256]{2,1,0:T(8,128)(2,1)} %param.5) | copy-start | bytes 1572868
  60.1 367.5 %copy-start.1 = (bf16[4096,256]{1,0:T(8,128)(2,1)}, bf16[4096,256]{1,0:T(8,128)(2,1)S(1)}, u32[]{:S(2)}) copy-start(bf16[4096,256]{1,0:T(8,128)(2,1)S(1)} %gather_fusion) | copy-start | bytes 6291460
  86.2 233.2 %all-reduce.15.cloned.1.call-start = ((), (), s32[]{:S(2)}) async-start(), calls=%async_computation.2 | async-start | bytes 524288 | tf_op jit(solution)/shard_map/psum | solution.py:33
  87.3 318.2 %all-reduce.13.cloned.1.call-start = ((), (), s32[]{:S(2)}) async-start(), calls=%async_computation.1 | async-start | bytes 1048576 | tf_op jit(solution)/shard_map/psum | solution.py:54
  189.2 3.0 copy-start.8
  189.2 216.4 %copy-start = (f32[512,256]{1,0:T(8,128)S(1)}, f32[512,256]{1,0:T(8,128)}, u32[]{:S(2)}) copy-start(f32[512,256]{1,0:T(8,128)} %all-reduce.11.cloned.1.call-done) | copy-start | bytes 1572868
  218.4 320.6 %all-reduce.17.cloned.1.call-start = ((), (), s32[]{:S(2)}) async-start(), calls=%async_computation.3 | async-start | bytes 1048576 | tf_op jit(solution)/shard_map/psum | solution.py:54
  407.4 0.8 copy-start.4
  424.5 114.5 %copy-start.3 = (f32[256,256]{1,0:T(8,128)S(1)}, f32[256,256]{1,0:T(8,128)}, u32[]{:S(2)}) copy-start(f32[256,256]{1,0:T(8,128)} %all-reduce.15.cloned.1.call-done) | copy-start | bytes 786436
  453.6 220.6 %all-reduce.19.cloned.1.call-start = ((), (), s32[]{:S(2)}) async-start(), calls=%async_computation.4 | async-start | bytes 1048576 | tf_op jit(solution)/shard_map/psum | solution.py:54
  589.0 218.8 %all-reduce.21.cloned.1.call-start = ((), (), s32[]{:S(2)}) async-start(), calls=%async_computation.5 | async-start | bytes 1048576 | tf_op jit(solution)/shard_map/psum | solution.py:54
  676.2 1.0 copy-start.6
  677.3 16.1 %copy-start.2 = (bf16[4096,256]{1,0:T(8,128)(2,1)S(1)}, bf16[4096,256]{1,0:T(8,128)(2,1)}, u32[]{:S(2)}) copy-start(bf16[4096,256]{1,0:T(8,128)(2,1)} %copy-done.1) | copy-start | bytes 6291460
  693.3 116.2 %copy-start.7 = (f32[512,256]{1,0:T(8,128)S(1)}, f32[512,256]{1,0:T(8,128)}, u32[]{:S(2)}) copy-start(f32[512,256]{1,0:T(8,128)} %copy-done.6) | copy-start | bytes 1572868
  722.5 218.7 %all-reduce.23.cloned.1.call-start = ((), (), s32[]{:S(2)}) async-start(), calls=%async_computation.6 | async-start | bytes 1048576 | tf_op jit(solution)/shard_map/psum | solution.py:54
  809.8 0.8 copy-start.5
  855.9 219.9 %all-reduce.25.cloned.1.call-start = ((), (), s32[]{:S(2)}) async-start(), calls=%async_computation.7 | async-start | bytes 1048576 | tf_op jit(solution)/shard_map/psum | solution.py:54
  990.5 218.8 %all-reduce.27.cloned.1.call-start = ((), (), s32[]{:S(2)}) async-start(), calls=%async_computation.8 | async-start | bytes 1048576 | tf_op jit(solution)/shard_map/psum | solution.py:54
  1124.0 218.8 %all-reduce.29.cloned.1.call-start = ((), (), s32[]{:S(2)}) async-start(), calls=%async_computation.9 | async-start | bytes 1048576 | tf_op jit(solution)/shard_map/psum | solution.py:54
Sparse Core Ops, SparseCore 0:
  9.7 34.5 all-gather.2
  86.3 85.7 all-reduce.10
  176.8 142.5 all-reduce.14
  322.5 83.0 all-reduce.12
  453.8 85.1 all-reduce.16
  589.2 85.0 all-reduce.18
  722.6 85.1 all-reduce.20
  856.0 85.1 all-reduce.22
  990.6 85.1 all-reduce.24
  1124.1 85.1 all-reduce.26
  1257.6 85.1 all-reduce.28
where the time goes:
time: 1360 us; the launch traced here: 1350 us
  waiting for transfers between devices  901 us (66%)
  other arithmetic  273 us (20%)
  local copies, waits for them, and re-layouts  147 us (11%)
  between operations  15.1 us (1%)
  matrix products  14.8 us (1%)
    psum x8, waiting for transfers between devices, image_every(): summed = lax.psum(local_terms(direction), 'ublk')  682 us
    scatter-add x8, other arithmetic, local_terms(): jax.ops.segment_sum(along[:, None] * rows, items, num_segments=column_items)  210 us
    gather x8, local copies, waits for them, and re-layouts, local_terms(): along = jnp.sum(rows * whole_dir[items], axis=1) * weight  130 us
    psum x1, waiting for transfers between devices, body(): gram = lax.psum(own_gram, ('ublk', 'salt'))  101 us
    psum x1, waiting for transfers between devices, body(): rhs = lax.psum(rhs_terms, 'ublk')  84.7 us
    all_gather x1, waiting for transfers between devices, body(): block = lax.all_gather(shard, 'salt', axis=0, tiled=True)  33.5 us
  transfers between devices with their start and end apart: 11, of which 11 were waited for; matrix products, arithmetic and copies ran while one was open for 4% of the time, Pallas kernels for 0%

commit v1 on v0

--- a/solution.py
+++ b/solution.py
@@ -7,6 +7,10 @@
 ITEM_DEV = 32
 REG = 1.0
 EPS = 1e-06
+
+
+def pools_step_on(arr):
+    return jnp.sum(lax.all_gather(arr, "ublk"), axis=0)
 
 
 def conjugate(rhs, image_of):
@@ -51,7 +55,7 @@
     rhs = lax.psum(rhs_terms, "ublk")
 
     def image_every(direction):
-        summed = lax.psum(local_terms(direction), "ublk")
+        summed = pools_step_on(local_terms(direction))
         return finish(summed, direction)
 
     solution_all, resid_all = conjugate(rhs, image_every)

time: 1360 us -> 1260 us (0.926)
  waiting for transfers between devices: 901 us -> 774 us
  other arithmetic: 273 us -> 304 us
    psum x8 -> x0, waiting for transfers between devices: 682 us -> none  [image_every(): summed = lax.psum(local_terms(direction), 'ublk')]
    all_gather x0 -> x8, waiting for transfers between devices: none -> 560 us  [pools_step_on(): return jnp.sum(lax.all_gather(arr, 'ublk'), axis=0)]
    reduce_sum x0 -> x8, other arithmetic: none -> 33.7 us  [pools_step_on(): return jnp.sum(lax.all_gather(arr, 'ublk'), axis=0)]
  transfers between devices with their start and end apart: 11 -> 11, of which waited for: 11 -> 11; matrix products, arithmetic and copies ran while one was open for 4% -> 1% of each run, Pallas kernels for 0% -> 0%
where the time goes in v1:
time: 1260 us; the launch traced here: 1250 us
  waiting for transfers between devices  774 us (61%)
  other arithmetic  304 us (24%)
  local copies, waits for them, and re-layouts  147 us (12%)
  between operations  16.9 us (1%)
    all_gather x8, waiting for transfers between devices, pools_step_on(): return jnp.sum(lax.all_gather(arr, 'ublk'), axis=0)  560 us
    scatter-add x8, other arithmetic, local_terms(): jax.ops.segment_sum(along[:, None] * rows, items, num_segments=column_items)  210 us
    gather x8, local copies, waits for them, and re-layouts, local_terms(): along = jnp.sum(rows * whole_dir[items], axis=1) * weight  130 us
    psum x1, waiting for transfers between devices, body(): gram = lax.psum(own_gram, ('ublk', 'salt'))  93.7 us
    psum x1, waiting for transfers between devices, body(): rhs = lax.psum(rhs_terms, 'ublk')  85.8 us
    reduce_sum x8, other arithmetic, pools_step_on(): return jnp.sum(lax.all_gather(arr, 'ublk'), axis=0)  33.7 us
    all_gather x1, waiting for transfers between devices, body(): block = lax.all_gather(shard, 'salt', axis=0, tiled=True)  33.5 us
    scatter-add x1, other arithmetic, body(): jax.ops.segment_sum(confid[:, None] * rows, items, num_segments=column_it...  26.1 us
  transfers between devices with their start and end apart: 11, of which 11 were waited for; matrix products, arithmetic and copies ran while one was open for 1% of the time, Pallas kernels for 0%

profile of v1, /device:TPU:0, one launch (start us, length us, event | category | flops | bytes accessed | tf_op | source)
XLA Modules:
  0.0 1253.0 jit_solution(13004228726509729796)
XLA Ops:
  11.6 33.5 %all-gather.19.cloned.1.call-done = bf16[1,8192,256]{2,1,0:T(8,128)(2,1)} async-done(((bf16[1,1024,256]{2,1,0:T(8,128)(2,1)}), bf16[1,8192,256]{2,1,0:T(8,128)(2,1)}) %all-gather.19.cloned.1.call-update) | async-done | bytes 4194320 | tf_op jit(solution)/shard_map/all_gather | solution.py:34
  60.9 26.1 %scatter_custom_fusion = f32[512,256]{1,0:T(8,128)} fusion(s32[4096]{0:T(1024)S(1)} %bitcast.72, f32[4096]{0:T(1024)S(1)} %add_select_fusion, f32[]{:T(128)} %constant.11.clone.1, bf16[4096,256]{1,0:T(8,128)(2,1)S(1)} %gather_fusion, pred[4096]{0:T(1024)(128)(4,1)S(1)} %compare_and_fusion), kind=kCustom, calls=%fused_computation.35 | custom fusion | flops 4194304 | bytes 2641924 | tf_op jit(solution)/shard_map/scatter-add | solution.py:46
  87.1 85.8 %all-reduce.3.cloned.1.call-done = f32[512,256]{1,0:T(8,128)} async-done(((f32[512,256]{1,0:T(8,128)}), f32[512,256]{1,0:T(8,128)}) %all-reduce.3.cloned.1.call-update) | async-done | bytes 524304 | tf_op jit(solution)/shard_map/psum | solution.py:55
  172.9 17.1 %gather_fusion.1 = f32[4096,256]{1,0:T(8,128)} fusion(f32[512,256]{1,0:T(8,128)} %all-reduce.3.cloned.1.call-done, s32[4096]{0:T(1024)S(1)} %broadcast_clamp_fusion), kind=kCustom, calls=%fused_computation.1 | custom fusion | bytes 8404992 | tf_op jit(solution)/shard_map/gather | solution.py:49
  193.0 26.1 %scatter_custom_fusion.1 = f32[512,256]{1,0:T(8,128)} fusion(s32[4096]{0:T(1024)S(1)} %bitcast.73, f32[4096]{0:T(1024)S(1)} %fusion.60, f32[]{:T(128)} %constant.11.clone.1, bf16[4096,256]{1,0:T(8,128)(2,1)S(1)} %gather_fusion, pred[4096]{0:T(1024)(128)(4,1)S(1)} %compare_and_fusion), kind=kCustom, calls=%fused_computation.37 | custom fusion | flops 4194304 | bytes 2641924 | tf_op jit(solution)/shard_map/scatter-add | solution.py:50
  220.8 68.8 %all-gather.21.cloned.1.call-done = f32[8192,256]{1,0:T(8,128)} async-done(((f32[512,256]{1,0:T(8,128)}), f32[8192,256]{1,0:T(8,128)}) %all-gather.21.cloned.1.call-update) | async-done | bytes 8388624 | tf_op jit(solution)/shard_map/all_gather | solution.py:13
  293.7 93.7 %all-reduce.5.cloned.1.call-done = f32[256,256]{1,0:T(8,128)} async-done(((f32[256,256]{1,0:T(8,128)}), f32[256,256]{1,0:T(8,128)}) %all-reduce.5.cloned.1.call-update) | async-done | bytes 262160 | tf_op jit(solution)/shard_map/psum | solution.py:37
  390.2 16.1 %gather_fusion.2 = f32[4096,256]{1,0:T(8,128)} fusion(f32[512,256]{1,0:T(8,128)S(1)} %multiply_add_fusion.7, s32[4096]{0:T(1024)S(1)} %broadcast_clamp_fusion), kind=kCustom, calls=%fused_computation.2 | custom fusion | bytes 8404992 | tf_op jit(solution)/shard_map/gather | solution.py:49
  409.2 26.1 %scatter_custom_fusion.2 = f32[512,256]{1,0:T(8,128)} fusion(s32[4096]{0:T(1024)S(1)} %bitcast.74, f32[4096]{0:T(1024)S(1)} %fusion.59, f32[]{:T(128)} %constant.11.clone.1, bf16[4096,256]{1,0:T(8,128)(2,1)S(1)} %gather_fusion, pred[4096]{0:T(1024)(128)(4,1)S(1)} %compare_and_fusion), kind=kCustom, calls=%fused_computation.39 | custom fusion | flops 4194304 | bytes 2641924 | tf_op jit(solution)/shard_map/scatter-add | solution.py:50
  435.4 68.2 %all-gather.23.cloned.1.call-done = f32[8192,256]{1,0:T(8,128)} async-done(((f32[512,256]{1,0:T(8,128)}), f32[8192,256]{1,0:T(8,128)}) %all-gather.23.cloned.1.call-update) | async-done | bytes 8388624 | tf_op jit(solution)/shard_map/all_gather | solution.py:13
  509.6 16.1 %gather_fusion.3 = f32[4096,256]{1,0:T(8,128)} fusion(f32[512,256]{1,0:T(8,128)S(1)} %multiply_add_fusion.5, s32[4096]{0:T(1024)S(1)} %broadcast_clamp_fusion), kind=kCustom, calls=%fused_computation.3 | custom fusion | bytes 8404992 | tf_op jit(solution)/shard_map/gather | solution.py:49
  529.1 26.5 %scatter_custom_fusion.3 = f32[512,256]{1,0:T(8,128)} fusion(s32[4096]{0:T(1024)S(1)} %bitcast.75, f32[4096]{0:T(1024)S(1)} %fusion.58, f32[]{:T(128)} %constant.11.clone.1, bf16[4096,256]{1,0:T(8,128)(2,1)} %copy-done.1, pred[4096]{0:T(1024)(128)(4,1)S(1)} %compare_and_fusion), kind=kCustom, calls=%fused_computation.41 | custom fusion | flops 4194304 | bytes 2641924 | tf_op jit(solution)/shard_map/scatter-add | solution.py:50
  555.9 70.4 %all-gather.25.cloned.1.call-done = f32[8192,256]{1,0:T(8,128)} async-done(((f32[512,256]{1,0:T(8,128)}), f32[8192,256]{1,0:T(8,128)}) %all-gather.25.cloned.1.call-update) | async-done | bytes 8388624 | tf_op jit(solution)/shard_map/all_gather | solution.py:13
  651.3 26.1 %scatter_custom_fusion.4 = f32[512,256]{1,0:T(8,128)} fusion(s32[4096]{0:T(1024)S(1)} %bitcast.76, f32[4096]{0:T(1024)S(1)} %fusion.57, f32[]{:T(128)} %constant.11.clone.1, bf16[4096,256]{1,0:T(8,128)(2,1)S(1)} %copy-done.2, pred[4096]{0:T(1024)(128)(4,1)S(1)} %compare_and_fusion), kind=kCustom, calls=%fused_computation.43 | custom fusion | flops 4194304 | bytes 2641924 | tf_op jit(solution)/shard_map/scatter-add | solution.py:50
  677.5 70.6 %all-gather.27.cloned.1.call-done = f32[8192,256]{1,0:T(8,128)} async-done(((f32[512,256]{1,0:T(8,128)}), f32[8192,256]{1,0:T(8,128)}) %all-gather.27.cloned.1.call-update) | async-done | bytes 8388624 | tf_op jit(solution)/shard_map/all_gather | solution.py:13
  774.9 26.1 %scatter_custom_fusion.5 = f32[512,256]{1,0:T(8,128)} fusion(s32[4096]{0:T(1024)S(1)} %bitcast.77, f32[4096]{0:T(1024)S(1)} %fusion.56, f32[]{:T(128)} %constant.11.clone.1, bf16[4096,256]{1,0:T(8,128)(2,1)S(1)} %copy-done.2, pred[4096]{0:T(1024)(128)(4,1)S(1)} %compare_and_fusion), kind=kCustom, calls=%fused_computation.45 | custom fusion | flops 4194304 | bytes 2641924 | tf_op jit(solution)/shard_map/scatter-add | solution.py:50
  801.3 70.4 %all-gather.29.cloned.1.call-done = f32[8192,256]{1,0:T(8,128)} async-done(((f32[512,256]{1,0:T(8,128)}), f32[8192,256]{1,0:T(8,128)}) %all-gather.29.cloned.1.call-update) | async-done | bytes 8388624 | tf_op jit(solution)/shard_map/all_gather | solution.py:13
  876.8 16.1 %gather_fusion.6 = f32[4096,256]{1,0:T(8,128)} fusion(f32[512,256]{1,0:T(8,128)S(1)} %multiply_add_fusion.2, s32[4096]{0:T(1024)S(1)} %broadcast_clamp_fusion), kind=kCustom, calls=%fused_computation.6 | custom fusion | bytes 8404992 | tf_op jit(solution)/shard_map/gather | solution.py:49
  896.4 26.5 %scatter_custom_fusion.6 = f32[512,256]{1,0:T(8,128)} fusion(s32[4096]{0:T(1024)S(1)} %bitcast.78, f32[4096]{0:T(1024)S(1)} %fusion.55, f32[]{:T(128)} %constant.11.clone.1, bf16[4096,256]{1,0:T(8,128)(2,1)} %copy-done.1, pred[4096]{0:T(1024)(128)(4,1)S(1)} %compare_and_fusion), kind=kCustom, calls=%fused_computation.47 | custom fusion | flops 4194304 | bytes 2641924 | tf_op jit(solution)/shard_map/scatter-add | solution.py:50
  923.0 70.6 %all-gather.31.cloned.1.call-done = f32[8192,256]{1,0:T(8,128)} async-done(((f32[512,256]{1,0:T(8,128)}), f32[8192,256]{1,0:T(8,128)}) %all-gather.31.cloned.1.call-update) | async-done | bytes 8388624 | tf_op jit(solution)/shard_map/all_gather | solution.py:13
  1018.2 26.5 %scatter_custom_fusion.7 = f32[512,256]{1,0:T(8,128)} fusion(s32[4096]{0:T(1024)S(1)} %bitcast.79, f32[4096]{0:T(1024)S(1)} %fusion.54, f32[]{:T(128)} %constant.11.clone.1, bf16[4096,256]{1,0:T(8,128)(2,1)} %copy-done.1, pred[4096]{0:T(1024)(128)(4,1)S(1)} %compare_and_fusion), kind=kCustom, calls=%fused_computation.49 | custom fusion | flops 4194304 | bytes 2641924 | tf_op jit(solution)/shard_map/scatter-add | solution.py:50
  1045.0 70.4 %all-gather.33.cloned.1.call-done = f32[8192,256]{1,0:T(8,128)} async-done(((f32[512,256]{1,0:T(8,128)}), f32[8192,256]{1,0:T(8,128)}) %all-gather.33.cloned.1.call-update) | async-done | bytes 8388624 | tf_op jit(solution)/shard_map/all_gather | solution.py:13
  1140.0 26.5 %scatter_custom_fusion.8 = f32[512,256]{1,0:T(8,128)} fusion(s32[4096]{0:T(1024)S(1)} %bitcast.80, f32[4096]{0:T(1024)S(1)} %fusion.53, f32[]{:T(128)} %constant.11.clone.1, bf16[4096,256]{1,0:T(8,128)(2,1)} %copy-done.1, pred[4096]{0:T(1024)(128)(4,1)S(1)} %compare_and_fusion), kind=kCustom, calls=%fused_computation.51 | custom fusion | flops 4194304 | bytes 2641924 | tf_op jit(solution)/shard_map/scatter-add | solution.py:50
  1166.9 70.4 %all-gather.35.cloned.1.call-done = f32[8192,256]{1,0:T(8,128)} async-done(((f32[512,256]{1,0:T(8,128)}), f32[8192,256]{1,0:T(8,128)}) %all-gather.35.cloned.1.call-update) | async-done | bytes 8388624 | tf_op jit(solution)/shard_map/all_gather | solution.py:13
  (127 shorter events, 161.4 us)
Async XLA Ops:
  8.0 37.1 %all-gather.19.cloned.1.call-start = ((), (), s32[]{:S(2)}) async-start(), calls=%async_computation.2 | async-start | bytes 4718592 | tf_op jit(solution)/shard_map/all_gather | solution.py:34
  8.7 164.1 %all-reduce.3.cloned.1.call-start = ((), (), s32[]{:S(2)}) async-start(), calls=%async_computation | async-start | bytes 1048576 | tf_op jit(solution)/shard_map/psum | solution.py:55
  45.1 15.8 %copy-start.12 = (s32[1,1,4096]{2,1,0:T(1,128)S(1)}, s32[1,1,4096]{2,1,0:T(1,128)}, u32[]{:S(2)}) copy-start(s32[1,1,4096]{2,1,0:T(1,128)} %param.7) | copy-start | bytes 49156
  60.8 348.4 %copy-start.1 = (bf16[4096,256]{1,0:T(8,128)(2,1)}, bf16[4096,256]{1,0:T(8,128)(2,1)S(1)}, u32[]{:S(2)}) copy-start(bf16[4096,256]{1,0:T(8,128)(2,1)S(1)} %gather_fusion) | copy-start | bytes 6291460
  87.0 202.7 %all-gather.21.cloned.1.call-start = ((), (), s32[]{:S(2)}) async-start(), calls=%async_computation.3 | async-start | bytes 8912896 | tf_op jit(solution)/shard_map/all_gather | solution.py:13
  190.0 3.0 copy-start.10
  190.0 29.2 %copy-start.11 = (bf16[1,1024,256]{2,1,0:T(8,128)(2,1)S(1)}, bf16[1,1024,256]{2,1,0:T(8,128)(2,1)}, u32[]{:S(2)}) copy-start(bf16[1,1024,256]{2,1,0:T(8,128)(2,1)} %param.5) | copy-start | bytes 1572868
  219.2 168.3 %all-reduce.5.cloned.1.call-start = ((), (), s32[]{:S(2)}) async-start(), calls=%async_computation.1 | async-start | bytes 524288 | tf_op jit(solution)/shard_map/psum | solution.py:37
  220.3 283.4 %all-gather.23.cloned.1.call-start = ((), (), s32[]{:S(2)}) async-start(), calls=%async_computation.4 | async-start | bytes 8912896 | tf_op jit(solution)/shard_map/all_gather | solution.py:13
  289.7 97.8 %copy-start = (f32[512,256]{1,0:T(8,128)S(1)}, f32[512,256]{1,0:T(8,128)}, u32[]{:S(2)}) copy-start(f32[512,256]{1,0:T(8,128)} %all-reduce.3.cloned.1.call-done) | copy-start | bytes 1572868
  389.1 0.8 copy-start.4
  435.4 191.0 %all-gather.25.cloned.1.call-start = ((), (), s32[]{:S(2)}) async-start(), calls=%async_computation.5 | async-start | bytes 8912896 | tf_op jit(solution)/shard_map/all_gather | solution.py:13
  503.6 4.1 copy-start.3
  503.6 4.7 copy-start.5
  555.7 192.5 %all-gather.27.cloned.1.call-start = ((), (), s32[]{:S(2)}) async-start(), calls=%async_computation.6 | async-start | bytes 8912896 | tf_op jit(solution)/shard_map/all_gather | solution.py:13
  631.3 1.0 copy-start.8
  632.3 16.1 %copy-start.2 = (bf16[4096,256]{1,0:T(8,128)(2,1)S(1)}, bf16[4096,256]{1,0:T(8,128)(2,1)}, u32[]{:S(2)}) copy-start(bf16[4096,256]{1,0:T(8,128)(2,1)} %copy-done.1) | copy-start | bytes 6291460
  677.5 194.2 %all-gather.29.cloned.1.call-start = ((), (), s32[]{:S(2)}) async-start(), calls=%async_computation.7 | async-start | bytes 8912896 | tf_op jit(solution)/shard_map/all_gather | solution.py:13
  748.1 6.6 copy-start.9
  754.9 0.8 copy-start.6
  801.1 192.5 %all-gather.31.cloned.1.call-start = ((), (), s32[]{:S(2)}) async-start(), calls=%async_computation.8 | async-start | bytes 8912896 | tf_op jit(solution)/shard_map/all_gather | solution.py:13
  871.7 4.7 copy-start.7
  922.9 192.5 %all-gather.33.cloned.1.call-start = ((), (), s32[]{:S(2)}) async-start(), calls=%async_computation.9 | async-start | bytes 8912896 | tf_op jit(solution)/shard_map/all_gather | solution.py:13
  1044.7 192.5 %all-gather.35.cloned.1.call-start = ((), (), s32[]{:S(2)}) async-start(), calls=%async_computation.10 | async-start | bytes 8912896 | tf_op jit(solution)/shard_map/all_gather | solution.py:13
Sparse Core Ops, SparseCore 0:
  10.5 34.5 all-gather.18
  87.1 85.7 all-reduce.2
  219.3 70.3 all-gather.20
  435.5 68.1 all-gather.22
  555.8 70.4 all-gather.24
  677.6 70.4 all-gather.26
  801.2 70.4 all-gather.28
  923.0 70.4 all-gather.30
  1044.9 70.4 all-gather.32
  1166.7 70.4 all-gather.34
Sparse Core Ops, SparseCore 1:
  224.4 163.0 all-reduce.4
